TPU v7x, 128 devices: a whole 4x4x4 slice. The times are simulated.
128 devices in a mesh: gx: 8 (over y, core), gy: 16 (over z, x).
Axes of the slice: x: 4, y: 4, z: 4, core: 2. Of those that a mesh axis runs over, the one named last changes fastest.
Arguments:
- right_side: float32 [128, 512, 256], P('gx', 'gy'), may hold values from -30 to 30
- start_field: float32 [128, 512, 256], P('gx', 'gy'), may hold values from -1.8 to 1.8
- coef: float32 [128, 512, 256], P('gx', 'gy'), may hold values from 0.5 to 2
- deflation: float32 [8, 128, 512, 256], P(None, 'gx', 'gy'), may hold values from -9 to 9
Outputs:
- solution: float32 [128, 512, 256], P('gx', 'gy')
- residual: float32 [128, 512, 256], P('gx', 'gy')
- direction: float32 [128, 512, 256], P('gx', 'gy')
All inputs are finite; a program needn't handle non-finite values.
Results may differ from a plain program's by a relative error of at most 0.0003.
Values sent between devices are 32-bit elements; how exact they have to be, the bound alone decides.
A program may use at most 192 MiB of HBM per device.

v0:
```python
import jax
import jax.numpy as jnp
from jax import lax
from jax.sharding import PartitionSpec as P

ITERS = 2
highest = lax.Precision.HIGHEST


def extended(cells, sides, width):
    for axis, dim in sides:
        count = lax.axis_size(axis)
        ends = count - 1
        head = lax.slice_in_dim(cells, 0, width, axis=dim)
        tail = lax.slice_in_dim(cells, cells.shape[dim] - width, cells.shape[dim], axis=dim)
        cells = jnp.concatenate(
            [
                lax.ppermute(tail, axis, [(i, (i + 1) % count) for i in range(ends)]),
                cells,
                lax.ppermute(head, axis, [((i + 1) % count, i) for i in range(ends)]),
            ],
            axis=dim,
        )
    return cells


def face_coef(padded, along):
    length = padded.shape[along]
    lower_side = lax.slice_in_dim(padded, 0, length - 1, axis=along)
    upper_side = lax.slice_in_dim(padded, 1, length, axis=along)
    inside = (lower_side > 0.0) & (upper_side > 0.0)
    summed = lower_side + upper_side
    return jnp.where(inside, 2.0 * lower_side * upper_side / summed, summed)


def block_operate(vectors, face_rows, face_cols, face_depth, diagonal):
    padded = jnp.pad(vectors, ((0, 0), (1, 1), (1, 1), (1, 1)))
    beside = face_rows[1:] * padded[:, 2:, 1:-1, 1:-1] + face_rows[:-1] * padded[:, :-2, 1:-1, 1:-1]
    beside = (
        beside
        + face_cols[:, 1:] * padded[:, 1:-1, 2:, 1:-1]
        + face_cols[:, :-1] * padded[:, 1:-1, :-2, 1:-1]
    )
    beside = (
        beside
        + face_depth[:, :, 1:] * padded[:, 1:-1, 1:-1, 2:]
        + face_depth[:, :, :-1] * padded[:, 1:-1, 1:-1, :-2]
    )
    return diagonal * vectors - beside


def face_product(lower_part, weights, upper_part):
    return -jnp.einsum("kab,lab->kl", lower_part * weights, upper_part, precision=highest)


def place(selector, blocks):
    return selector.astype(jnp.float32)[:, None, :, None] * blocks[:, :, None, :]


def block_masks(block_count, across):
    positions = jnp.arange(block_count, dtype=jnp.int32)
    row_ids = positions[:, None]
    col_ids = positions[None, :]
    self_mask = row_ids == col_ids
    below_rows = col_ids == row_ids - across
    below_cols = (col_ids == row_ids - 1) & (row_ids % across != 0)
    above_rows = col_ids == row_ids + across
    above_cols = (col_ids == row_ids + 1) & (col_ids % across != 0)
    return (self_mask, below_rows, below_cols, above_rows, above_cols)


def per_device(right_side, start_field, coef, deflation):
    num_vectors = deflation.shape[0]
    across = lax.axis_size("gy")
    block_count = lax.axis_size("gx") * across
    own_block = lax.axis_index("gx") * across + lax.axis_index("gy")
    padded = extended(coef, (("gx", 0), ("gy", 1)), 1)
    face_rows = face_coef(padded[:, 1:-1], 0)
    face_cols = face_coef(padded[1:-1], 1)
    face_depth = face_coef(jnp.pad(coef, ((0, 0), (0, 0), (1, 1))), 2)
    diagonal = face_rows[1:] + face_rows[:-1] + face_cols[:, 1:] + face_cols[:, :-1]
    diagonal = diagonal + face_depth[:, :, 1:] + face_depth[:, :, :-1]

    def apply_operator(values):
        rimmed_values = extended(values, (("gx", 0), ("gy", 1)), 1)
        depth_padded = jnp.pad(values, ((0, 0), (0, 0), (1, 1)))
        beside = face_rows[1:] * rimmed_values[2:, 1:-1] + face_rows[:-1] * rimmed_values[:-2, 1:-1]
        beside = (
            beside
            + face_cols[:, 1:] * rimmed_values[1:-1, 2:]
            + face_cols[:, :-1] * rimmed_values[1:-1, :-2]
        )
        beside = (
            beside
            + face_depth[:, :, 1:] * depth_padded[:, :, 2:]
            + face_depth[:, :, :-1] * depth_padded[:, :, :-2]
        )
        return diagonal * values - beside

    acted_on = block_operate(deflation, face_rows, face_cols, face_depth, diagonal)
    diag_block = jnp.einsum("kxyz,lxyz->kl", deflation, acted_on, precision=highest)
    rimmed = extended(deflation, (("gx", 1), ("gy", 2)), 1)
    below_rows = face_product(deflation[:, 0], face_rows[0], rimmed[:, 0, 1:-1])
    below_cols = face_product(deflation[:, :, 0], face_cols[:, 0], rimmed[:, 1:-1, 0])
    above_rows = face_product(deflation[:, -1], face_rows[-1], rimmed[:, -1, 1:-1])
    above_cols = face_product(deflation[:, :, -1], face_cols[:, -1], rimmed[:, 1:-1, -1])
    blocks = jnp.stack([diag_block, below_rows, below_cols, above_rows, above_cols])[None]
    gathered = lax.all_gather(blocks, ("gx", "gy"), axis=0, tiled=True)
    self_mask, mask_below_rows, mask_below_cols, mask_above_rows, mask_above_cols = block_masks(
        block_count, across
    )
    matrix = (
        place(self_mask, gathered[:, 0])
        + place(mask_below_rows, gathered[:, 1])
        + place(mask_below_cols, gathered[:, 2])
    )
    matrix = (
        matrix + place(mask_above_rows, gathered[:, 3]) + place(mask_above_cols, gathered[:, 4])
    )
    matrix = matrix.reshape(block_count * num_vectors, block_count * num_vectors)
    factor = jnp.linalg.cholesky(matrix)

    def solve_coarse(gathered_rows):
        flattened = gathered_rows.reshape(-1)
        solved = jax.scipy.linalg.cho_solve((factor, True), flattened)
        return lax.dynamic_slice_in_dim(solved, own_block * num_vectors, num_vectors)

    def restrict(values):
        return jnp.einsum("kxyz,xyz->k", deflation, values, precision=highest)

    def prolong(coarse_values):
        return jnp.einsum("kxyz,k->xyz", deflation, coarse_values, precision=highest)

    def coarse_plain(values):
        gathered_rows = lax.all_gather(restrict(values)[None], ("gx", "gy"), axis=0, tiled=True)
        return prolong(solve_coarse(gathered_rows))

    def coarse_with(values, residual_now, precond_now):
        inner_sum = lax.psum(jnp.sum(residual_now * precond_now), ("gx", "gy"))
        return (coarse_plain(values), inner_sum)

    solution = start_field + coarse_plain(right_side - apply_operator(start_field))
    residual = right_side - apply_operator(solution)
    precond = residual / diagonal
    correction, inner_now = coarse_with(apply_operator(precond), residual, precond)
    direction = precond - correction
    for iteration in range(ITERS):
        applied = apply_operator(direction)
        step_size = inner_now / lax.psum(jnp.sum(direction * applied), ("gx", "gy"))
        solution = solution + step_size * direction
        residual = residual - step_size * applied
        precond = residual / diagonal
        correction, inner_next = coarse_with(apply_operator(precond), residual, precond)
        direction = precond + inner_next / inner_now * direction - correction
        inner_now = inner_next
    return (solution, residual, direction)


def solution(mesh):
    placed = (
        P("gx", "gy", None),
        P("gx", "gy", None),
        P("gx", "gy", None),
        P(None, "gx", "gy", None),
    )
    return jax.shard_map(
        per_device,
        mesh=mesh,
        in_specs=placed,
        out_specs=(P("gx", "gy", None), P("gx", "gy", None), P("gx", "gy", None)),
        check_vma=False,
    )
```

profile of v0, /device:TPU:1, one launch (start us, length us, event | category | flops | bytes accessed | tf_op | source)
XLA Modules:
  0.0 1258.0 jit_solution(12469603402888341044)
XLA Ops:
  68.2 14.7 %fusion.6 = f32[8,16,32,256]{3,2,1,0:T(8,128)} fusion(f32[8,16,32,256]{3,2,1,0:T(8,128)} %param.9, f32[16,32,256]{2,1,0:T(8,128)} %copy.73, f32[16,32,256]{2,1,0:T(8,128)} %copy.72, f32[16,32,256]{2,1,0:T(8,128)} %copy.71, f32[16,32,256]{2,1,0:T(8,128)} %copy.70, f32[16,32,256]{2,1,0:T(8,128)} %copy.69, f32[16,32,256]{2,1,0:T(8,128)} %copy.68, ...), kind=kLoop, calls=%fused_computation.16 | loop fusion | flops 13631488 | bytes 12058624 | tf_op jit(solution)/shard_map/sub | solution.py:49
  82.9 15.8 %fusion.15 = f32[8,8]{0,1:T(8,128)} fusion(f32[8,16,32,256]{3,2,1,0:T(8,128)} %fusion.6, f32[8,16,32,256]{3,2,1,0:T(8,128)} %param.9), kind=kOutput, calls=%fused_computation.42 | convolution fusion | flops 100663296 | bytes 8388864 | tf_op jit(solution)/shard_map/kxyz,lxyz->kl/dot_general | solution.py:101
  100.1 12.9 %convolution_bitcast_fusion.23 = f32[8]{0:T(128)} fusion(f32[16,32,256,1]{2,0,1,3:T(8,128)S(1)} %copy-done.28, f32[8,16,32,256]{3,2,1,0:T(8,128)} %param.9), kind=kOutput, calls=%fused_computation.78 | convolution fusion | flops 12582912 | bytes 4718624 | tf_op jit(solution)/shard_map/kxyz,xyz->k/dot_general | solution.py:129
  113.9 72.3 %all-reduce.10 = f32[1024]{0:T(1024)} all-reduce(f32[1024]{0:T(1024)S(1)} %dynamic-update-slice.50), channel_id=3, replica_groups=mesh['gx'=8,'gy'=16] {'gx','gy'}, use_global_device_ids=true, to_apply=%add.10 | all-reduce | flops 1024 | bytes 8192
  196.5 69.1 %all-gather = f32[640,8,8]{2,1,0:T(8,128)S(1)} all-gather(f32[5,8,8]{2,1,0:T(8,128)S(1)} %fusion.20), channel_id=2, replica_groups=mesh['gx'=8,'gy'=16] {'gx','gy'}, dimensions={0}, use_global_device_ids=true | all-gather | bytes 165120 | tf_op jit(solution)/shard_map/all_gather | solution.py:108
  265.9 31.1 %multiply_add_fusion = f32[128,8,128,8]{3,2,1,0:T(8,128)} fusion(f32[128,8,8]{2,1,0:T(8,128)S(1)} %get-tuple-element.76, f32[128,128]{1,0:T(8,128)S(1)} %copy-done.36, f32[128,8,8]{2,1,0:T(8,128)S(1)} %get-tuple-element.77, f32[128,128]{1,0:T(8,128)S(1)} %copy-done.34, f32[128,8,8]{2,1,0:T(8,128)S(1)} %get-tuple-element.78, f32[128,128]{1,0:T(8,128)S(1)} %copy-done.35, ...), kind=kLoop, calls=%fused_computation.2 | loop fusion | flops 9437184 | bytes 4685824 | tf_op jit(solution)/shard_map/add | solution.py:118
  297.0 48.3 %reshape.508 = f32[1024,1024]{1,0:T(8,128)} reshape(f32[128,8,128,8]{3,2,1,0:T(8,128)} %multiply_add_fusion) | data formatting | bytes 8388608 | tf_op jit(solution)/shard_map/add | solution.py:118
  357.3 11.7 cholesky.226
  371.6 9.8 custom-call.64
  385.4 11.9 cholesky.247
  399.2 9.8 custom-call.65
  412.3 11.7 cholesky.474
  425.4 9.8 custom-call.66
  438.7 12.1 cholesky.493
  452.1 9.8 custom-call.67
  465.3 11.7 cholesky.512
  478.4 9.9 custom-call.68
  491.6 11.7 cholesky.532
  504.6 9.8 custom-call.69
  517.5 11.9 cholesky.552
  530.7 9.8 custom-call.70
  543.2 11.7 cholesky.570
  566.3 28.1 %while.8 = (s32[]{:T(128)}, f32[1024,1024]{1,0:T(8,128)}, s32[8,2]{0,1:T(2,128)S(1)}, f32[8,128,128]{2,1,0:T(8,128)}, s32[]{:T(128)}) while((s32[]{:T(128)}, f32[1024,1024]{1,0:T(8,128)}, s32[8,2]{0,1:T(2,128)S(1)}, f32[8,128,128]{2,1,0:T(8,128)}, s32[]{:T(128)}) %tuple.176), condition=%wide.while_cond, body=%wide.while_body.sunk | while | flops 2 | bytes 132705 | solution.py:125
  594.3 79.8 %custom-call.74 = f32[8,128,128]{1,2,0:T(8,128)S(1)} custom-call(f32[8,128,128]{2,1,0:T(8,128)} %get-tuple-element.30), custom_call_target="InvertDiagBlocksLowerTriangular" | custom-call | tf_op jit(solution)/shard_map/jit(_cho_solve)/triangular_solve | solution.py:125
  732.1 10.9 convolution_bitcast_fusion.18
  743.2 69.9 %all-reduce.11 = f32[1024]{0:T(1024)S(1)} all-reduce(f32[1024]{0:T(1024)S(1)} %dynamic-update-slice.51), channel_id=4, replica_groups=mesh['gx'=8,'gy'=16] {'gx','gy'}, use_global_device_ids=true, to_apply=%add.11 | all-reduce | flops 1024 | bytes 8192
  854.7 68.3 %all-reduce.16 = (f32[]{:T(128)}, f32[]{:T(128)}) all-reduce(f32[]{:T(128)} %get-tuple-element.64, f32[]{:T(128)} %get-tuple-element.62), channel_id=1, replica_groups=mesh['gx'=8,'gy'=16] {'gx','gy'}, use_global_device_ids=true, to_apply=%region_17.19 | all-reduce | flops 2 | bytes 16 | tf_op jit(solution)/shard_map/psum | solution.py:139
  940.5 10.6 convolution_bitcast_fusion.13
  951.3 68.2 %all-reduce.15 = (f32[1024]{0:T(1024)S(1)}, f32[]{:T(128)}) all-reduce(f32[1024]{0:T(1024)S(1)} %dynamic-update-slice.52, f32[]{:T(128)} %get-tuple-element.59), channel_id=5, replica_groups=mesh['gx'=8,'gy'=16] {'gx','gy'}, use_global_device_ids=true, to_apply=%add.12 | all-reduce | flops 1025 | bytes 8200
  1062.6 68.1 %psum.38 = f32[]{:T(128)} all-reduce(f32[]{:T(128)} %get-tuple-element.57), channel_id=1, replica_groups=mesh['gx'=8,'gy'=16] {'gx','gy'}, use_global_device_ids=true, to_apply=%region_23.25 | all-reduce | flops 1 | bytes 8 | tf_op jit(solution)/shard_map/psum | solution.py:149
  1148.1 10.6 convolution_bitcast_fusion.8
  1159.0 68.0 %all-reduce.14 = (f32[1024]{0:T(1024)S(1)}, f32[]{:T(128)}) all-reduce(f32[1024]{0:T(1024)S(1)} %dynamic-update-slice.53, f32[]{:T(128)} %get-tuple-element.54), channel_id=6, replica_groups=mesh['gx'=8,'gy'=16] {'gx','gy'}, use_global_device_ids=true, to_apply=%add.13 | all-reduce | flops 1025 | bytes 8200
  (522 shorter events, 363.0 us)
Async XLA Ops:
  2.1 42.5 %collective-permute-start = (f32[1,32,256]{2,0,1:T(1,128)}, f32[1,32,256]{2,0,1:T(1,128)}, u32[]{:S(2)}, u32[]{:S(2)}) collective-permute-start(f32[1,32,256]{2,0,1:T(1,128)} %copy.61), channel_id=1, source_target_pairs={{0,16},{16,32},{32,48},{48,64},{64,80},{80,96},{96,112},{1,17},{17... | collective-permute-start | bytes 98312 | tf_op jit(solution)/shard_map/ppermute | solution.py:18
  7.3 33.5 %collective-permute-start.1 = (f32[1,32,256]{2,0,1:T(1,128)}, f32[1,32,256]{2,0,1:T(1,128)}, u32[]{:S(2)}, u32[]{:S(2)}) collective-permute-start(f32[1,32,256]{2,0,1:T(1,128)} %copy.63), channel_id=1, source_target_pairs={{16,0},{32,16},{48,32},{64,48},{80,64},{96,80},{112,96},{17,1},{33... | collective-permute-start | bytes 98312 | tf_op jit(solution)/shard_map/ppermute | solution.py:20
  10.6 39.3 %collective-permute-start.8 = (f32[1,32,256]{2,0,1:T(1,128)}, f32[1,32,256]{2,0,1:T(1,128)}, u32[]{:S(2)}, u32[]{:S(2)}) collective-permute-start(f32[1,32,256]{2,0,1:T(1,128)} %copy.87), channel_id=1, source_target_pairs={{16,0},{32,16},{48,32},{64,48},{80,64},{96,80},{112,96},{17,1},{33... | collective-permute-start | bytes 98312 | tf_op jit(solution)/shard_map/ppermute | solution.py:20
  13.2 38.1 %collective-permute-start.9 = (f32[1,32,256]{2,0,1:T(1,128)}, f32[1,32,256]{2,0,1:T(1,128)}, u32[]{:S(2)}, u32[]{:S(2)}) collective-permute-start(f32[1,32,256]{2,0,1:T(1,128)} %copy.89), channel_id=1, source_target_pairs={{0,16},{16,32},{32,48},{48,64},{64,80},{80,96},{96,112},{1,17},{17... | collective-permute-start | bytes 98312 | tf_op jit(solution)/shard_map/ppermute | solution.py:18
  23.4 163.6 %collective-permute-start.4 = (f32[8,1,32,256]{3,0,2,1:T(8,128)}, f32[8,1,32,256]{3,0,2,1:T(8,128)S(1)}, u32[]{:S(2)}, u32[]{:S(2)}) collective-permute-start(f32[8,1,32,256]{3,0,2,1:T(8,128)} %slice.817), channel_id=1, source_target_pairs={{0,16},{16,32},{32,48},{48,64},{64,80},{80,96},{96,112},{1,17},{17... | collective-permute-start | bytes 786440 | tf_op jit(solution)/shard_map/ppermute | solution.py:18
  40.8 146.1 %collective-permute-start.5 = (f32[8,1,32,256]{3,0,1,2:T(8,128)}, f32[8,1,32,256]{3,0,1,2:T(8,128)}, u32[]{:S(2)}, u32[]{:S(2)}) collective-permute-start(f32[8,1,32,256]{3,0,1,2:T(8,128)} %slice.815), channel_id=1, source_target_pairs={{16,0},{32,16},{48,32},{64,48},{80,64},{96,80},{112,96},{17,1},{33... | collective-permute-start | bytes 786440 | tf_op jit(solution)/shard_map/ppermute | solution.py:20
  46.8 9.9 collective-permute-start.2
  50.0 11.3 collective-permute-start.3
  51.9 11.2 collective-permute-start.10
  56.7 6.4 collective-permute-start.11
  188.0 4.2 collective-permute-start.6
  189.3 6.8 collective-permute-start.7
  701.2 5.6 collective-permute-start.12
  707.8 5.3 collective-permute-start.14
  709.1 4.9 collective-permute-start.15
  716.3 7.3 collective-permute-start.16
  719.3 5.3 collective-permute-start.17
  724.6 6.0 collective-permute-start.18
  725.9 5.5 collective-permute-start.19
  839.8 5.7 collective-permute-start.20
  842.3 4.1 collective-permute-start.21
  846.5 5.3 collective-permute-start.22
  847.8 5.0 collective-permute-start.23
  927.1 5.6 collective-permute-start.24
  933.7 5.7 collective-permute-start.26
  935.0 4.9 collective-permute-start.27
  1047.8 5.6 collective-permute-start.28
  1054.3 5.3 collective-permute-start.30
  1055.6 4.9 collective-permute-start.31
  1134.4 5.6 collective-permute-start.32
  1141.0 6.6 collective-permute-start.34
  1142.3 5.3 collective-permute-start.35
  (46 other events, 1195.3 us)
where the time goes:
time: 1270 us; the launch traced here: 1260 us
  blocking collectives  484 us (38%)
  other arithmetic  334 us (26%)
  matrix products  192 us (15%)
  local copies, waits for them, and re-layouts  126 us (10%)
  starting transfers between devices  97.7 us (8%)
  between operations  13.1 us (1%)
    unnamed x4, blocking collectives  278 us
    another operation x31, other arithmetic, per_device(): factor = jnp.linalg.cholesky(matrix)  173 us
    another operation x4, other arithmetic, solve_coarse(): solved = jax.scipy.linalg.cho_solve((factor, True), flattened)  85.2 us
    another operation x120, matrix products, solve_coarse(): solved = jax.scipy.linalg.cho_solve((factor, True), flattened)  83.1 us
    all_gather x1, blocking collectives, per_device(): gathered = lax.all_gather(blocks, ('gx', 'gy'), axis=0, tiled=True)  69.1 us
    psum x1, blocking collectives, coarse_with(): inner_sum = lax.psum(jnp.sum(residual_now * precond_now), ('gx', 'gy'))  68.3 us
    psum x1, blocking collectives, per_device(): step_size = inner_now / lax.psum(jnp.sum(direction * applied), ('gx', 'gy'))  68.1 us
    ppermute x18, starting transfers between devices, extended(): lax.ppermute(tail, axis, [(i, (i + 1) % count) for i in range(ends)])  63.2 us
  transfers between devices with their start and end apart: 36, of which 12 were waited for; matrix products, arithmetic and copies ran while one was open for 7% of the time, Pallas kernels for 0%

commit v1 on v0

--- a/solution.py
+++ b/solution.py
@@ -105,7 +105,10 @@
     above_rows = face_product(deflation[:, -1], face_rows[-1], rimmed[:, -1, 1:-1])
     above_cols = face_product(deflation[:, :, -1], face_cols[:, -1], rimmed[:, 1:-1, -1])
     blocks = jnp.stack([diag_block, below_rows, below_cols, above_rows, above_cols])[None]
-    gathered = lax.all_gather(blocks, ("gx", "gy"), axis=0, tiled=True)
+    gathered = jnp.concatenate(
+        lax.all_to_all(jnp.stack([blocks] * lax.axis_size(("gx", "gy"))), ("gx", "gy"), 0, 0),
+        axis=0,
+    )
     self_mask, mask_below_rows, mask_below_cols, mask_above_rows, mask_above_cols = block_masks(
         block_count, across
     )

time: 1270 us -> 1230 us (0.969)
  blocking collectives: 484 us -> 410 us
  starting transfers between devices: 97.7 us -> 119 us
    all_gather x1 -> x0, blocking collectives: 69.1 us -> none  [per_device(): gathered = lax.all_gather(blocks, ('gx', 'gy'), axis=0, tiled=True)]
    all_to_all x0 -> x1, starting transfers between devices: none -> 19.2 us  [per_device(): lax.all_to_all(jnp.stack([blocks] * lax.axis_size(('gx', 'gy'))), ('gx',...]
  transfers between devices with their start and end apart: 36 -> 37, of which waited for: 12 -> 12; matrix products, arithmetic and copies ran while one was open for 7% -> 7% of each run, Pallas kernels for 0% -> 0%
where the time goes in v1:
time: 1230 us; the launch traced here: 1210 us
  blocking collectives  410 us (33%)
  other arithmetic  334 us (27%)
  matrix products  190 us (15%)
  local copies, waits for them, and re-layouts  134 us (11%)
  starting transfers between devices  119 us (10%)
  between operations  12.8 us (1%)
    unnamed x4, blocking collectives  274 us
    another operation x31, other arithmetic, per_device(): factor = jnp.linalg.cholesky(matrix)  173 us
    another operation x4, other arithmetic, solve_coarse(): solved = jax.scipy.linalg.cho_solve((factor, True), flattened)  85.2 us
    another operation x120, matrix products, solve_coarse(): solved = jax.scipy.linalg.cho_solve((factor, True), flattened)  83.1 us
    psum x1, blocking collectives, coarse_with(): inner_sum = lax.psum(jnp.sum(residual_now * precond_now), ('gx', 'gy'))  68 us
    psum x1, blocking collectives, per_device(): step_size = inner_now / lax.psum(jnp.sum(direction * applied), ('gx', 'gy'))  67.9 us
    ppermute x18, starting transfers between devices, extended(): lax.ppermute(tail, axis, [(i, (i + 1) % count) for i in range(ends)])  65.7 us
    add x2, local copies, waits for them, and re-layouts, per_device(): matrix + place(mask_above_rows, gathered[:, 3])  53.8 us
  transfers between devices with their start and end apart: 37, of which 12 were waited for; matrix products, arithmetic and copies ran while one was open for 7% of the time, Pallas kernels for 0%

profile of v1, /device:TPU:1, one launch (start us, length us, event | category | flops | bytes accessed | tf_op | source)
XLA Modules:
  0.0 1211.3 jit_solution(13465531051411022679)
XLA Ops:
  68.2 14.7 %fusion.6 = f32[8,16,32,256]{3,2,1,0:T(8,128)} fusion(f32[8,16,32,256]{3,2,1,0:T(8,128)} %param.9, f32[16,32,256]{2,1,0:T(8,128)} %copy.69, f32[16,32,256]{2,1,0:T(8,128)} %copy.68, f32[16,32,256]{2,1,0:T(8,128)} %copy.67, f32[16,32,256]{2,1,0:T(8,128)} %copy.66, f32[16,32,256]{2,1,0:T(8,128)} %copy.65, f32[16,32,256]{2,1,0:T(8,128)} %copy.64, ...), kind=kLoop, calls=%fused_computation.16 | loop fusion | flops 13631488 | bytes 12058624 | tf_op jit(solution)/shard_map/sub | solution.py:49
  83.0 15.2 %fusion.15 = f32[8,8]{0,1:T(8,128)S(1)} fusion(f32[8,16,32,256]{3,2,1,0:T(8,128)} %fusion.6, f32[8,16,32,256]{3,2,1,0:T(8,128)} %param.9), kind=kOutput, calls=%fused_computation.42 | convolution fusion | flops 100663296 | bytes 8388864 | tf_op jit(solution)/shard_map/kxyz,lxyz->kl/dot_general | solution.py:101
  115.1 19.2 %all-to-all-start = ((f32[128,1,320]{2,1,0:T(1,128)}), f32[128,1,320]{2,1,0:T(1,128)S(1)}, u32[]{:S(2)}, u32[]{:S(2)}) async-start(f32[128,1,320]{2,1,0:T(1,128)} %reshape.876), calls=%async_computation | async-start | bytes 393216 | tf_op jit(solution)/shard_map/all_to_all | solution.py:109
  134.4 12.0 convolution_bitcast_fusion.23
  146.6 67.1 %all-reduce.10 = f32[1024]{0:T(1024)S(1)} all-reduce(f32[1024]{0:T(1024)S(1)} %dynamic-update-slice.50), channel_id=2, replica_groups=mesh['gx'=8,'gy'=16] {'gx','gy'}, use_global_device_ids=true, to_apply=%add.10 | all-reduce | flops 1024 | bytes 8192
  219.7 31.1 %multiply_add_fusion = f32[128,8,128,8]{3,2,1,0:T(8,128)} fusion(f32[128,8,8]{2,1,0:T(8,128)S(1)} %get-tuple-element.76, f32[128,128]{1,0:T(8,128)S(1)} %copy-done.35, f32[128,8,8]{2,1,0:T(8,128)S(1)} %get-tuple-element.77, f32[128,128]{1,0:T(8,128)S(1)} %copy-done.33, f32[128,8,8]{2,1,0:T(8,128)S(1)} %get-tuple-element.78, f32[128,128]{1,0:T(8,128)S(1)} %copy-done.34, ...), kind=kLoop, calls=%fused_computation.2 | loop fusion | flops 9437184 | bytes 4685824 | tf_op jit(solution)/shard_map/add | solution.py:121
  250.8 48.3 %reshape.514 = f32[1024,1024]{1,0:T(8,128)} reshape(f32[128,8,128,8]{3,2,1,0:T(8,128)} %multiply_add_fusion) | data formatting | bytes 8388608 | tf_op jit(solution)/shard_map/add | solution.py:121
  311.1 11.7 cholesky.226
  325.4 9.8 custom-call.64
  339.1 11.9 cholesky.247
  352.9 9.8 custom-call.65
  366.1 11.7 cholesky.474
  379.1 9.8 custom-call.66
  392.4 12.1 cholesky.493
  405.8 9.8 custom-call.67
  419.1 11.7 cholesky.512
  432.1 9.9 custom-call.68
  445.3 11.7 cholesky.532
  458.3 9.8 custom-call.69
  471.2 11.9 cholesky.552
  484.4 9.8 custom-call.70
  496.8 11.7 cholesky.570
  519.7 28.0 %while.8 = (s32[]{:T(128)}, f32[1024,1024]{1,0:T(8,128)}, s32[8,2]{0,1:T(2,128)S(1)}, f32[8,128,128]{2,1,0:T(8,128)}, s32[]{:T(128)}) while((s32[]{:T(128)}, f32[1024,1024]{1,0:T(8,128)}, s32[8,2]{0,1:T(2,128)S(1)}, f32[8,128,128]{2,1,0:T(8,128)}, s32[]{:T(128)}) %tuple.176), condition=%wide.while_cond, body=%wide.while_body.sunk | while | flops 2 | bytes 132705 | solution.py:128
  547.8 79.8 %custom-call.74 = f32[8,128,128]{1,2,0:T(8,128)S(1)} custom-call(f32[8,128,128]{2,1,0:T(8,128)} %get-tuple-element.30), custom_call_target="InvertDiagBlocksLowerTriangular" | custom-call | tf_op jit(solution)/shard_map/jit(_cho_solve)/triangular_solve | solution.py:128
  685.6 10.9 convolution_bitcast_fusion.18
  696.7 70.0 %all-reduce.11 = f32[1024]{0:T(1024)S(1)} all-reduce(f32[1024]{0:T(1024)S(1)} %dynamic-update-slice.51), channel_id=3, replica_groups=mesh['gx'=8,'gy'=16] {'gx','gy'}, use_global_device_ids=true, to_apply=%add.11 | all-reduce | flops 1024 | bytes 8192
  808.2 68.0 %all-reduce.16 = (f32[]{:T(128)}, f32[]{:T(128)}) all-reduce(f32[]{:T(128)} %get-tuple-element.64, f32[]{:T(128)} %get-tuple-element.62), channel_id=1, replica_groups=mesh['gx'=8,'gy'=16] {'gx','gy'}, use_global_device_ids=true, to_apply=%region_17.19 | all-reduce | flops 2 | bytes 16 | tf_op jit(solution)/shard_map/psum | solution.py:142
  893.8 10.6 convolution_bitcast_fusion.13
  904.6 68.5 %all-reduce.15 = (f32[1024]{0:T(1024)S(1)}, f32[]{:T(128)}) all-reduce(f32[1024]{0:T(1024)S(1)} %dynamic-update-slice.52, f32[]{:T(128)} %get-tuple-element.59), channel_id=4, replica_groups=mesh['gx'=8,'gy'=16] {'gx','gy'}, use_global_device_ids=true, to_apply=%add.12 | all-reduce | flops 1025 | bytes 8200
  1016.2 67.9 %psum.38 = f32[]{:T(128)} all-reduce(f32[]{:T(128)} %get-tuple-element.57), channel_id=1, replica_groups=mesh['gx'=8,'gy'=16] {'gx','gy'}, use_global_device_ids=true, to_apply=%region_23.25 | all-reduce | flops 1 | bytes 8 | tf_op jit(solution)/shard_map/psum | solution.py:152
  1101.5 10.6 convolution_bitcast_fusion.8
  1112.4 68.1 %all-reduce.14 = (f32[1024]{0:T(1024)S(1)}, f32[]{:T(128)}) all-reduce(f32[1024]{0:T(1024)S(1)} %dynamic-update-slice.53, f32[]{:T(128)} %get-tuple-element.54), channel_id=5, replica_groups=mesh['gx'=8,'gy'=16] {'gx','gy'}, use_global_device_ids=true, to_apply=%add.13 | all-reduce | flops 1025 | bytes 8200
  (526 shorter events, 373.2 us)
Async XLA Ops:
  2.1 42.5 %collective-permute-start = (f32[1,32,256]{2,0,1:T(1,128)}, f32[1,32,256]{2,0,1:T(1,128)}, u32[]{:S(2)}, u32[]{:S(2)}) collective-permute-start(f32[1,32,256]{2,0,1:T(1,128)} %copy.57), channel_id=1, source_target_pairs={{0,16},{16,32},{32,48},{48,64},{64,80},{80,96},{96,112},{1,17},{17... | collective-permute-start | bytes 98312 | tf_op jit(solution)/shard_map/ppermute | solution.py:18
  7.3 33.6 %collective-permute-start.1 = (f32[1,32,256]{2,0,1:T(1,128)}, f32[1,32,256]{2,0,1:T(1,128)}, u32[]{:S(2)}, u32[]{:S(2)}) collective-permute-start(f32[1,32,256]{2,0,1:T(1,128)} %copy.59), channel_id=1, source_target_pairs={{16,0},{32,16},{48,32},{64,48},{80,64},{96,80},{112,96},{17,1},{33... | collective-permute-start | bytes 98312 | tf_op jit(solution)/shard_map/ppermute | solution.py:20
  10.6 39.3 %collective-permute-start.8 = (f32[1,32,256]{2,0,1:T(1,128)}, f32[1,32,256]{2,0,1:T(1,128)}, u32[]{:S(2)}, u32[]{:S(2)}) collective-permute-start(f32[1,32,256]{2,0,1:T(1,128)} %copy.83), channel_id=1, source_target_pairs={{16,0},{32,16},{48,32},{64,48},{80,64},{96,80},{112,96},{17,1},{33... | collective-permute-start | bytes 98312 | tf_op jit(solution)/shard_map/ppermute | solution.py:20
  13.2 38.0 %collective-permute-start.9 = (f32[1,32,256]{2,0,1:T(1,128)}, f32[1,32,256]{2,0,1:T(1,128)}, u32[]{:S(2)}, u32[]{:S(2)}) collective-permute-start(f32[1,32,256]{2,0,1:T(1,128)} %copy.85), channel_id=1, source_target_pairs={{0,16},{16,32},{32,48},{48,64},{64,80},{80,96},{96,112},{1,17},{17... | collective-permute-start | bytes 98312 | tf_op jit(solution)/shard_map/ppermute | solution.py:18
  23.3 75.0 %collective-permute-start.4 = (f32[8,1,32,256]{3,0,2,1:T(8,128)}, f32[8,1,32,256]{3,0,2,1:T(8,128)S(1)}, u32[]{:S(2)}, u32[]{:S(2)}) collective-permute-start(f32[8,1,32,256]{3,0,2,1:T(8,128)} %slice.817), channel_id=1, source_target_pairs={{0,16},{16,32},{32,48},{48,64},{64,80},{80,96},{96,112},{1,17},{17... | collective-permute-start | bytes 786440 | tf_op jit(solution)/shard_map/ppermute | solution.py:18
  40.9 57.5 %collective-permute-start.5 = (f32[8,1,32,256]{3,0,1,2:T(8,128)}, f32[8,1,32,256]{3,0,1,2:T(8,128)}, u32[]{:S(2)}, u32[]{:S(2)}) collective-permute-start(f32[8,1,32,256]{3,0,1,2:T(8,128)} %slice.815), channel_id=1, source_target_pairs={{16,0},{32,16},{48,32},{64,48},{80,64},{96,80},{112,96},{17,1},{33... | collective-permute-start | bytes 786440 | tf_op jit(solution)/shard_map/ppermute | solution.py:20
  46.8 9.9 collective-permute-start.2
  49.9 11.4 collective-permute-start.3
  52.0 11.2 collective-permute-start.10
  56.7 6.4 collective-permute-start.11
  99.4 6.8 collective-permute-start.6
  102.9 6.5 collective-permute-start.7
  115.1 98.6 %all-to-all-start = ((f32[128,1,320]{2,1,0:T(1,128)}), f32[128,1,320]{2,1,0:T(1,128)S(1)}, u32[]{:S(2)}, u32[]{:S(2)}) async-start(f32[128,1,320]{2,1,0:T(1,128)} %reshape.876), calls=%async_computation | async-start | bytes 393216 | tf_op jit(solution)/shard_map/all_to_all | solution.py:109
  654.7 5.6 collective-permute-start.12
  661.3 5.3 collective-permute-start.14
  662.6 4.9 collective-permute-start.15
  669.9 7.3 collective-permute-start.16
  672.4 5.8 collective-permute-start.17
  678.2 6.0 collective-permute-start.18
  679.5 5.5 collective-permute-start.19
  793.4 5.6 collective-permute-start.20
  800.0 5.3 collective-permute-start.22
  801.3 4.9 collective-permute-start.23
  880.4 5.6 collective-permute-start.24
  887.0 5.7 collective-permute-start.26
  888.3 4.9 collective-permute-start.27
  1001.4 5.6 collective-permute-start.28
  1008.0 5.3 collective-permute-start.30
  1009.3 4.9 collective-permute-start.31
  1087.8 5.6 collective-permute-start.32
  1094.3 6.6 collective-permute-start.34
  1095.6 5.3 collective-permute-start.35
  (46 other events, 638.2 us)
